TPU v7x, 32 devices: a whole 2x2x4 slice. The times are simulated.
32 devices in a mesh: space: 8 (over y, x, core), tm: 4 (over z).
Axes of the slice: x: 2, y: 2, z: 4, core: 2. Of those that a mesh axis runs over, the one named last changes fastest.
Arguments:
- state_anom: bfloat16 [4, 65536, 128], P('tm', 'space'), may hold values from -6 to 6
- obs_rows: bfloat16 [4, 16384, 128], P('tm', 'space'), may hold values from -6 to 6
- obs_weight: bfloat16 [4, 16384], P('tm', 'space'), may hold values from 0.0099487305 to 0.19921875
- innovation: bfloat16 [4, 16384], P('tm', 'space'), may hold values from -15 to 15
- obs_block: int32 [4, 16384, 1], P('tm', 'space'), may hold values from 0 to 15; in each aligned block of 2048 rows (0 to 2047, 2048 to 4095, ..., all dimensions but the last counted through in order) at most 256 rows name the same one
Outputs:
- smoothed: bfloat16 [4, 65536, 128], P('tm', 'space')
- increment: float32 [4, 65536], P('tm', 'space')
Inputs may be any that keep to these rules, and one draw needn't show every extreme that they name: `obs_block`: among the 2048 observations of one device (aligned blocks of 2048 along the observation dimension) at one time, no block is named more than 256 times, and some block is named exactly 256 times.
All inputs are finite; a program needn't handle non-finite values.
Results may differ from a plain program's by a relative error of at most 0.0049.
Values may be sent and summed in bfloat16 or wider, within the bound.
A program may use at most 64 MiB of HBM per device.

v0:
```python
import functools
import math

import jax
import jax.numpy as jnp
from jax import lax
from jax.experimental import pallas as pl
from jax.experimental.pallas import tpu as pltpu
from jax.sharding import PartitionSpec as P

BLK_DEV = 2
PAD = 8
MESH = pl.DeviceIdType.MESH
NT_DIMS = (((1,), (1,)), ((), ()))


def partner(me, k, n):
    out, bit = 0, 1
    while bit < n:
        out = out + bit * ((me // bit + k // bit) % 2)
        bit *= 2
    return out


def steps(low, high, body):
    if high - low <= 16:
        for k in range(low, high):
            body(k)
    else:
        lax.fori_loop(low, high, lambda k, c: (body(k), c)[1], 0)


def fold(gram, two):
    half = gram.shape[0] // 2
    wide = gram.shape[1]
    row = lax.broadcasted_iota(jnp.int32, (half, wide), 0)
    lane = lax.broadcasted_iota(jnp.int32, (half, wide), 1)
    low = gram[half:, :]
    main = jnp.where((lane > row) & (lane < half), pltpu.roll(low, half, 1), gram[0:half, :])
    diag = jnp.sum(jnp.where(lane == row + half, low, 0.0), axis=0, keepdims=True)
    return main, jnp.where(lax.broadcasted_iota(jnp.int32, (PAD, wide), 0) == PAD - 1, diag, two)


def gram_kernel(n, rows_ref, weight_ref, innov_ref, block_ref, anom_ref, out_ref, anom_out, anom_sem, scaled, drv, right, near, own, near_in, far_in, send_sem, recv_sem):
    me = lax.axis_index("space")
    members = rows_ref.shape[1]
    half = members // 2
    chips = n // 2
    barrier = pltpu.get_barrier_semaphore()

    def greet(k):
        pl.semaphore_signal(barrier, inc=1, device_id={"space": partner(me, k, n)}, device_id_type=MESH)

    greet(1)
    steps(1, chips, lambda q: greet(2 * q))
    fetch = pltpu.make_async_copy(anom_ref, anom_out, anom_sem)
    fetch.start()
    weight = weight_ref[...].astype(jnp.float32)
    rows_t = rows_ref[...].astype(jnp.float32).T
    scaled[...] = (weight * rows_t).astype(jnp.bfloat16)
    rows_t = rows_t.astype(jnp.bfloat16)
    for h in range(BLK_DEV):
        pick = jnp.where(block_ref[...] % BLK_DEV == h, 1.0, 0.0).astype(jnp.bfloat16)
        right[members * h:members * (h + 1), :] = rows_t * pick
    weighted = weight * innov_ref[...].astype(jnp.float32)
    high = weighted.astype(jnp.bfloat16)
    low = (weighted - high.astype(jnp.float32)).astype(jnp.bfloat16)
    drv[...] = jnp.concatenate(
        [high.astype(jnp.float32), low.astype(jnp.float32), jnp.zeros((2 * PAD - 2, high.shape[1]), jnp.float32)], axis=0
    ).astype(jnp.bfloat16)

    def parts(devs):
        lhs = []
        for dev in devs:
            mask = jnp.where(block_ref[...] // BLK_DEV == dev, 1.0, 0.0).astype(jnp.bfloat16)
            lhs = lhs + [scaled[...] * mask, drv[...] * mask]
        both = lax.dot_general(jnp.concatenate(lhs, axis=0), right[...], NT_DIMS, preferred_element_type=jnp.float32)
        for i in range(len(devs)):
            at = i * (members + 2 * PAD)
            yield [
                fold(both[at:at + members, members * h:members * (h + 1)],
                     both[at + members:at + members + PAD, members * h:members * (h + 1)])
                for h in range(BLK_DEV)
            ]

    def near_copy(q):
        return pltpu.make_async_remote_copy(
            src_ref=near.at[q], dst_ref=near_in.at[q], send_sem=send_sem.at[0, q], recv_sem=recv_sem.at[0, q],
            device_id={"space": partner(me, 1, n)}, device_id_type=MESH,
        )

    def far_copy(q):
        return pltpu.make_async_remote_copy(
            src_ref=own.at[q], dst_ref=far_in.at[q], send_sem=send_sem.at[1, q], recv_sem=recv_sem.at[1, q],
            device_id={"space": partner(me, 2 * q, n)}, device_id_type=MESH,
        )

    def work(q):
        for place, part in zip((near, own), parts((partner(me, 2 * q + 1, n), partner(me, 2 * q, n)))):
            for h, (main, rest) in enumerate(part):
                place[q, h, 0:half, :] = main
                place[q, h, half:, :] = rest

    def relay(q):
        near_copy(q).wait()
        own[q] = own[q] + near_in[q]
        far_copy(q).start()

    work(chips - 1)
    pl.semaphore_wait(barrier, chips)
    near_copy(chips - 1).start()

    def advance(turn):
        q = chips - 1 - turn
        work(q)
        near_copy(q).start()
        relay(q + 1)

    steps(1, chips, advance)
    near_copy(0).wait()
    out_ref[...] = own[0] + near_in[0]

    def take(turn):
        q = chips - turn
        far_copy(q).wait()
        out_ref[...] += far_in[q]

    steps(1, chips, take)
    fetch.wait()


def factor_kernel(n, sums_ref, total_ref, offset_ref, acc, off, tri, vec, tri_in, vec_in, send_sem, recv_sem):
    here = lax.axis_index("tm")
    barrier = pltpu.get_barrier_semaphore()

    def greet(k):
        pl.semaphore_signal(barrier, inc=1, device_id={"tm": (here + k) % n}, device_id_type=MESH)

    steps(1, n, greet)
    members = tri.shape[1]
    half = members // 2
    groups = members // 8
    lane = lax.broadcasted_iota(jnp.int32, (8, members), 1)
    sub_wide = lax.broadcasted_iota(jnp.int32, (8, members), 0)
    row = lax.broadcasted_iota(jnp.int32, (members, members), 0)
    col = lax.broadcasted_iota(jnp.int32, (members, members), 1)
    work, drive = [], []
    for h in range(BLK_DEV):
        main = sums_ref[h, 0:half, :]
        rest = sums_ref[h, half:, :]
        r0, c0 = row[0:half, :], col[0:half, :]
        top = jnp.where((c0 < r0) | (c0 >= half), main, 0.0)
        bottom = jnp.where(c0 > r0 + half, pltpu.roll(main, half, 1), 0.0)
        part = jnp.concatenate([top, bottom], axis=0)
        first = jnp.concatenate([main, jnp.broadcast_to(rest[PAD - 1:PAD, :], (half, members))], axis=0)
        system = part + part.T + jnp.where(row == col, first + (members - 1.0), 0.0)
        work.append([system[8 * g:8 * g + 8, :] for g in range(groups)])
        drive.append(rest[0:1, :] + rest[1:2, :])
    inverse = [[], []]
    for g0 in range(groups):
        base = 8 * g0
        place = sub_wide + base
        panel = (lane >= base) & (lane < base + 8)
        for h in range(BLK_DEV):
            w = work[h]
            z = jnp.where(panel, jnp.where(lane == place, 1.0, 0.0), w[g0])
            cols = [jnp.broadcast_to(w[g0][:, base + q:base + q + 1], (8, members)) for q in range(8)]
            kept, pivots = z, cols[0]
            for q in range(8):
                here_row = sub_wide == q
                kept = jnp.where(here_row, z, kept)
                pivots = jnp.where(here_row, cols[q], pivots)
                factor = jnp.where(here_row, 0.0, cols[q] * (1.0 / cols[q][q:q + 1, :]))
                z = z - factor * z[q:q + 1, :]
                for p in range(q + 1, 8):
                    cols[p] = cols[p] - factor * cols[p][q:q + 1, :]
            z = z * (1.0 / pivots)
            inverse[h].append(jnp.where(lane <= place, kept, 0.0) * lax.rsqrt(pivots))
            if g0 + 1 == groups:
                continue
            fresh = jnp.where(panel, 0.0, w[g0 + 1])
            for q in range(8):
                fresh = fresh - w[g0 + 1][:, base + q:base + q + 1] * z[q:q + 1, :]
            if g0 + 2 < groups:
                rest = jnp.concatenate(w[g0 + 2:], axis=0)
                wide = (col >= base)[0:members - base - 16, :] & (col < base + 8)[0:members - base - 16, :]
                deep = jnp.concatenate([jnp.zeros((8, members), jnp.float32)] * g0 + [z] + [jnp.zeros((8, members), jnp.float32)] * (groups - g0 - 1), axis=0)
                moved = jnp.dot(jnp.where(wide, rest, 0.0), deep, precision=lax.Precision.HIGHEST, preferred_element_type=jnp.float32)
                rest = jnp.where(wide, 0.0, rest) - moved
                for g in range(g0 + 2, groups):
                    w[g] = rest[8 * (g - g0 - 2):8 * (g - g0 - 1), :]
            w[g0 + 1] = fresh
    scale = math.sqrt(members - 1.0)
    packed, lines = jnp.zeros((members, members), jnp.float32), []
    for h in range(BLK_DEV):
        x = jnp.concatenate(inverse[h], axis=0)
        inner = jnp.sum(x * drive[h], axis=1, keepdims=True)
        shift = jnp.sum(x * inner, axis=0, keepdims=True)
        flip = x.T
        packed = packed + jnp.where(col < row, x, 0.0) if h == 0 else packed + jnp.where(col > row, flip, 0.0)
        lines = lines + [jnp.sum(jnp.where(row == col, x, 0.0), axis=0, keepdims=True), shift]
        acc[h] = scale * flip
        off[h] = jnp.sum(jnp.where(row == col, jnp.broadcast_to(shift, (members, members)), 0.0), axis=1, keepdims=True)
    tri[...] = packed.astype(jnp.bfloat16)
    vec[...] = jnp.concatenate(lines + [jnp.zeros((PAD - 2 * BLK_DEV, members), jnp.float32)], axis=0)
    pl.semaphore_wait(barrier, n - 1)

    def copies(k):
        peer = {"tm": (here + n - k) % n}
        return (
            pltpu.make_async_remote_copy(
                src_ref=tri, dst_ref=tri_in.at[k], send_sem=send_sem.at[0, k], recv_sem=recv_sem.at[0, k],
                device_id=peer, device_id_type=MESH,
            ),
            pltpu.make_async_remote_copy(
                src_ref=vec, dst_ref=vec_in.at[k], send_sem=send_sem.at[1, k], recv_sem=recv_sem.at[1, k],
                device_id=peer, device_id_type=MESH,
            ),
        )

    def push(k):
        @pl.when(here >= k)
        def _():
            for copy in copies(k):
                copy.start()

    steps(1, n, lambda turn: push(n - turn))

    def take(k):
        @pl.when(here + k < n)
        def _():
            for copy in copies(k):
                copy.wait_recv()
            got = tri_in[k].astype(jnp.float32)
            for h in range(BLK_DEV):
                before = acc[h]
                diag = vec_in[k, 2 * h:2 * h + 1, :]
                shift = vec_in[k, 2 * h + 1:2 * h + 2, :]
                off[h] = off[h] + jnp.sum(before * shift, axis=1, keepdims=True)
                high = before.astype(jnp.bfloat16)
                low = (before - high.astype(jnp.float32)).astype(jnp.bfloat16)
                pair = jnp.concatenate([high, low], axis=0)
                if h == 0:
                    side = jnp.where(col < row, got, 0.0).astype(jnp.bfloat16)
                    both = lax.dot_general(pair, side, NT_DIMS, preferred_element_type=jnp.float32)
                else:
                    side = jnp.where(col > row, got, 0.0).astype(jnp.bfloat16)
                    both = jnp.dot(pair, side, preferred_element_type=jnp.float32)
                acc[h] = scale * (before * diag + both[0:members, :] + both[members:, :])

    steps(1, n, take)

    def settle(k):
        @pl.when(here >= k)
        def _():
            for copy in copies(k):
                copy.wait_send()

    steps(1, n, settle)
    for h in range(BLK_DEV):
        total_ref[h] = acc[h].astype(jnp.bfloat16)
        spread = jnp.where(row == col, jnp.broadcast_to(off[h], (members, members)), 0.0)
        line = jnp.sum(spread, axis=0, keepdims=True)
        offset_ref[h] = jnp.broadcast_to(line, (16, members)).astype(jnp.bfloat16)


def apply_kernel(anom_ref, total_ref, offset_ref, smooth_ref, inc_ref, smooth, inc, sems):
    rows_dev = anom_ref.shape[1]
    tiles = 8
    tile = rows_dev // tiles
    out = []
    for i in range(tiles):
        h = i * BLK_DEV // tiles
        cut = slice(i * tile, (i + 1) * tile)
        anom = anom_ref[0, cut, :]
        smooth[0, cut, :] = jnp.dot(anom, total_ref[h], preferred_element_type=jnp.float32).astype(jnp.bfloat16)
        copy = pltpu.make_async_copy(smooth.at[:, cut, :], smooth_ref.at[:, cut, :], sems.at[i])
        copy.start()
        out.append(copy)
        part = lax.dot_general(offset_ref[h], anom, NT_DIMS, preferred_element_type=jnp.float32)
        inc[:, cut] = part[0:1, :]
    copy = pltpu.make_async_copy(inc, inc_ref, sems.at[tiles])
    copy.start()
    for copy in out + [copy]:
        copy.wait()


def body(state_anom, obs_rows, obs_weight, innovation, obs_block):
    count, members = obs_rows.shape[1:]
    n_space = lax.axis_size("space")
    n_time = lax.axis_size("tm")
    wide = members // 2 + PAD
    vmem = pl.BlockSpec(memory_space=pltpu.VMEM)
    sums, anom = pl.pallas_call(
        functools.partial(gram_kernel, n_space),
        out_shape=(
            jax.ShapeDtypeStruct((BLK_DEV, wide, members), jnp.float32),
            pltpu.VMEM(state_anom.shape, state_anom.dtype),
        ),
        in_specs=[vmem] * 4 + [pl.BlockSpec(memory_space=pl.ANY)],
        out_specs=(vmem, vmem),
        scratch_shapes=[
            pltpu.SemaphoreType.DMA(()),
            pltpu.VMEM((members, count), jnp.bfloat16),
            pltpu.VMEM((2 * PAD, count), jnp.bfloat16),
            pltpu.VMEM((BLK_DEV * members, count), jnp.bfloat16),
            *[pltpu.VMEM((n_space // 2, BLK_DEV, wide, members), jnp.float32)] * 4,
            pltpu.SemaphoreType.DMA((2, n_space // 2)),
            pltpu.SemaphoreType.DMA((2, n_space // 2)),
        ],
        compiler_params=pltpu.CompilerParams(collective_id=0, has_side_effects=True),
        name="gram",
    )(obs_rows[0], obs_weight, innovation, obs_block.reshape(1, count), state_anom)
    total, offset = pl.pallas_call(
        functools.partial(factor_kernel, n_time),
        out_shape=(
            jax.ShapeDtypeStruct((BLK_DEV, members, members), jnp.bfloat16),
            jax.ShapeDtypeStruct((BLK_DEV, 16, members), jnp.bfloat16),
        ),
        in_specs=[vmem],
        out_specs=(vmem, vmem),
        scratch_shapes=[
            pltpu.VMEM((BLK_DEV, members, members), jnp.float32),
            pltpu.VMEM((BLK_DEV, members, 1), jnp.float32),
            pltpu.VMEM((members, members), jnp.bfloat16),
            pltpu.VMEM((PAD, members), jnp.float32),
            pltpu.VMEM((n_time, members, members), jnp.bfloat16),
            pltpu.VMEM((n_time, PAD, members), jnp.float32),
            pltpu.SemaphoreType.DMA((2, n_time)),
            pltpu.SemaphoreType.DMA((2, n_time)),
        ],
        compiler_params=pltpu.CompilerParams(collective_id=1, has_side_effects=True),
        name="factor",
    )(sums)
    rows_dev = state_anom.shape[1]
    any_spec = pl.BlockSpec(memory_space=pl.ANY)
    return pl.pallas_call(
        apply_kernel,
        out_shape=(
            jax.ShapeDtypeStruct((1, rows_dev, members), jnp.bfloat16),
            jax.ShapeDtypeStruct((1, rows_dev), jnp.float32),
        ),
        in_specs=[vmem] * 3,
        out_specs=(any_spec, any_spec),
        scratch_shapes=[
            pltpu.VMEM((1, rows_dev, members), jnp.bfloat16),
            pltpu.VMEM((1, rows_dev), jnp.float32),
            pltpu.SemaphoreType.DMA((9,)),
        ],
        name="apply",
    )(pltpu.with_memory_space_constraint(anom, pltpu.MemorySpace.VMEM), total, offset)


def solution(mesh):
    placed = (
        P("tm", "space", None),
        P("tm", "space", None),
        P("tm", "space"),
        P("tm", "space"),
        P("tm", "space", None),
    )
    return jax.shard_map(
        body,
        mesh=mesh,
        in_specs=placed,
        out_specs=(P("tm", "space", None), P("tm", "space")),
        check_vma=False,
    )
```

profile of v0, /device:TPU:0, one launch (start us, length us, event | category | flops | bytes accessed | tf_op | source)
XLA Modules:
  0.0 27.9 jit_solution(12039764153015795976)
XLA Ops:
  0.6 12.0 %gram.1 = (f32[2,72,128]{2,1,0:T(8,128)}, bf16[1,8192,128]{2,1,0:T(8,128)(2,1)S(1)}) custom-call(bf16[2048,128]{1,0:T(8,128)(2,1)} %bitcast.2, bf16[1,2048]{1,0:T(2,128)(2,1)} %weight_ref.1, bf16[1,2048]{1,0:T(2,128)(2,1)} %innov_ref.1, s32[1,2048]{1,0:T(1,128)} %bitcast.3, bf16[1,8192,128]{2,1,0:T(8,128)(2,1)} %anom_ref.1), custom_call_target="tpu_custom_call" | custom-call | tf_op jit(solution)/shard_map/gram/pallas_call | solution.py:294
  12.7 12.4 %factor.1 = (bf16[2,128,128]{2,1,0:T(8,128)(2,1)}, bf16[2,16,128]{2,1,0:T(8,128)(2,1)}) custom-call(f32[2,72,128]{2,1,0:T(8,128)} %get-tuple-element.7.sums_ref), custom_call_target="tpu_custom_call" | custom-call | tf_op jit(solution)/shard_map/factor/pallas_call | solution.py:314
  25.1 2.9 %apply.1 = (bf16[1,8192,128]{2,1,0:T(8,128)(2,1)}, f32[1,8192]{1,0:T(1,128)}) custom-call(bf16[1,8192,128]{2,1,0:T(8,128)(2,1)S(1)} %get-tuple-element.6.anom_ref, bf16[2,128,128]{2,1,0:T(8,128)(2,1)} %get-tuple-element.8.total_ref, bf16[2,16,128]{2,1,0:T(8,128)(2,1)} %get-tuple-element.9.offset_ref), custom_call_target="tpu_custom_call" | custom-call | tf_op jit(solution)/shard_map/apply/pallas_call | solution.py:337
where the time goes:
time: 28.1 us; the launch traced here: 27.9 us
  Pallas kernels  27.3 us (97%)
  between operations  0.65 us (2%)
    pallas_call x1, Pallas kernels, body(): pl.pallas_call(functools.partial(factor_kernel, n_time), out_shape=(jax.S...  12.4 us
    pallas_call x1, Pallas kernels, body(): pl.pallas_call(functools.partial(gram_kernel, n_space), out_shape=(jax.Sh...  12 us
    pallas_call x1, Pallas kernels, body(): pl.pallas_call(apply_kernel, out_shape=(jax.ShapeDtypeStruct((1, rows_dev...  2.85 us

commit v1 on v0

--- a/solution.py
+++ b/solution.py
@@ -10,6 +10,8 @@
 
 BLK_DEV = 2
 PAD = 8
+GRANT = 24 * 1024 * 1024
+GRAM_GRANT = 64696320
 MESH = pl.DeviceIdType.MESH
 NT_DIMS = (((1,), (1,)), ((), ()))
 
@@ -41,7 +43,15 @@
     return main, jnp.where(lax.broadcasted_iota(jnp.int32, (PAD, wide), 0) == PAD - 1, diag, two)
 
 
-def gram_kernel(n, rows_ref, weight_ref, innov_ref, block_ref, anom_ref, out_ref, anom_out, anom_sem, scaled, drv, right, near, own, near_in, far_in, send_sem, recv_sem):
+def gram_kernel(n, rows_hbm, weight_hbm, innov_hbm, block_hbm, anom_ref, out_ref, anom_out, anom_sem, rows_ref, weight_ref, innov_ref, block_ref, in_sem, scaled, drv, right, near, own, near_in, far_in, send_sem, recv_sem):
+    loads = [
+        pltpu.make_async_copy(src, dst, in_sem.at[i])
+        for i, (src, dst) in enumerate(
+            ((rows_hbm, rows_ref), (weight_hbm, weight_ref), (innov_hbm, innov_ref), (block_hbm, block_ref))
+        )
+    ]
+    for load in loads:
+        load.start()
     me = lax.axis_index("space")
     members = rows_ref.shape[1]
     half = members // 2
@@ -55,6 +65,8 @@
     steps(1, chips, lambda q: greet(2 * q))
     fetch = pltpu.make_async_copy(anom_ref, anom_out, anom_sem)
     fetch.start()
+    for load in loads:
+        load.wait()
     weight = weight_ref[...].astype(jnp.float32)
     rows_t = rows_ref[...].astype(jnp.float32).T
     scaled[...] = (weight * rows_t).astype(jnp.bfloat16)
@@ -294,13 +306,18 @@
     sums, anom = pl.pallas_call(
         functools.partial(gram_kernel, n_space),
         out_shape=(
-            jax.ShapeDtypeStruct((BLK_DEV, wide, members), jnp.float32),
+            pltpu.VMEM((BLK_DEV, wide, members), jnp.float32),
             pltpu.VMEM(state_anom.shape, state_anom.dtype),
         ),
-        in_specs=[vmem] * 4 + [pl.BlockSpec(memory_space=pl.ANY)],
+        in_specs=[pl.BlockSpec(memory_space=pltpu.MemorySpace.HBM)] * 5,
         out_specs=(vmem, vmem),
         scratch_shapes=[
             pltpu.SemaphoreType.DMA(()),
+            pltpu.VMEM((count, members), obs_rows.dtype),
+            pltpu.VMEM((1, count), obs_weight.dtype),
+            pltpu.VMEM((1, count), innovation.dtype),
+            pltpu.VMEM((1, count), obs_block.dtype),
+            pltpu.SemaphoreType.DMA((4,)),
             pltpu.VMEM((members, count), jnp.bfloat16),
             pltpu.VMEM((2 * PAD, count), jnp.bfloat16),
             pltpu.VMEM((BLK_DEV * members, count), jnp.bfloat16),
@@ -308,14 +325,14 @@
             pltpu.SemaphoreType.DMA((2, n_space // 2)),
             pltpu.SemaphoreType.DMA((2, n_space // 2)),
         ],
-        compiler_params=pltpu.CompilerParams(collective_id=0, has_side_effects=True),
+        compiler_params=pltpu.CompilerParams(collective_id=0, has_side_effects=True, vmem_limit_bytes=GRAM_GRANT),
         name="gram",
     )(obs_rows[0], obs_weight, innovation, obs_block.reshape(1, count), state_anom)
     total, offset = pl.pallas_call(
         functools.partial(factor_kernel, n_time),
         out_shape=(
-            jax.ShapeDtypeStruct((BLK_DEV, members, members), jnp.bfloat16),
-            jax.ShapeDtypeStruct((BLK_DEV, 16, members), jnp.bfloat16),
+            pltpu.VMEM((BLK_DEV, members, members), jnp.bfloat16),
+            pltpu.VMEM((BLK_DEV, 16, members), jnp.bfloat16),
         ),
         in_specs=[vmem],
         out_specs=(vmem, vmem),
@@ -329,9 +346,9 @@
             pltpu.SemaphoreType.DMA((2, n_time)),
             pltpu.SemaphoreType.DMA((2, n_time)),
         ],
-        compiler_params=pltpu.CompilerParams(collective_id=1, has_side_effects=True),
+        compiler_params=pltpu.CompilerParams(collective_id=1, has_side_effects=True, vmem_limit_bytes=GRANT),
         name="factor",
-    )(sums)
+    )(pltpu.with_memory_space_constraint(sums, pltpu.MemorySpace.VMEM))
     rows_dev = state_anom.shape[1]
     any_spec = pl.BlockSpec(memory_space=pl.ANY)
     return pl.pallas_call(
@@ -347,8 +364,9 @@
             pltpu.VMEM((1, rows_dev), jnp.float32),
             pltpu.SemaphoreType.DMA((9,)),
         ],
+        compiler_params=pltpu.CompilerParams(vmem_limit_bytes=GRANT),
         name="apply",
-    )(pltpu.with_memory_space_constraint(anom, pltpu.MemorySpace.VMEM), total, offset)
+    )(*[pltpu.with_memory_space_constraint(x, pltpu.MemorySpace.VMEM) for x in (anom, total, offset)])
 
 
 def solution(mesh):

time: 28.1 us -> 25.1 us (0.89)
  Pallas kernels: 27.3 us -> 24.3 us
    pallas_call x2, Pallas kernels: 24.4 us -> 22.2 us  [the longest x1 11.3 us: body(): pl.pallas_call(functools.partial(gram_kernel, n_space), out_shape=(pltpu....]
    pallas_call x1, Pallas kernels: 2.85 us -> 2.02 us  [body(): pl.pallas_call(apply_kernel, out_shape=(jax.ShapeDtypeStruct((1, rows_dev...]
where the time goes in v1:
time: 25.1 us; the launch traced here: 24.9 us
  Pallas kernels  24.3 us (97%)
  between operations  0.65 us (3%)
    pallas_call x1, Pallas kernels, body(): pl.pallas_call(functools.partial(gram_kernel, n_space), out_shape=(pltpu....  11.3 us
    pallas_call x1, Pallas kernels, body(): pl.pallas_call(functools.partial(factor_kernel, n_time), out_shape=(pltpu...  10.9 us
    pallas_call x1, Pallas kernels, body(): pl.pallas_call(apply_kernel, out_shape=(jax.ShapeDtypeStruct((1, rows_dev...  2.02 us

profile of v1, /device:TPU:0, one launch (start us, length us, event | category | flops | bytes accessed | tf_op | source)
XLA Modules:
  0.0 24.9 jit_solution(12663994636375935475)
XLA Ops:
  0.6 11.3 %gram.1 = (f32[2,72,128]{2,1,0:T(8,128)S(1)}, bf16[1,8192,128]{2,1,0:T(8,128)(2,1)S(1)}) custom-call(bf16[2048,128]{1,0:T(8,128)(2,1)} %bitcast.2, bf16[1,2048]{1,0:T(2,128)(2,1)} %weight_hbm.1, bf16[1,2048]{1,0:T(2,128)(2,1)} %innov_hbm.1, s32[1,2048]{1,0:T(1,128)} %bitcast.3, bf16[1,8192,128]{2,1,0:T(8,128)(2,1)} %anom_ref.1), custom_call_target="tpu_custom_call" | custom-call | tf_op jit(solution)/shard_map/gram/pallas_call | solution.py:306
  12.0 10.9 %factor.1 = (bf16[2,128,128]{2,1,0:T(8,128)(2,1)S(1)}, bf16[2,16,128]{2,1,0:T(8,128)(2,1)S(1)}) custom-call(f32[2,72,128]{2,1,0:T(8,128)S(1)} %get-tuple-element.7.sums_ref), custom_call_target="tpu_custom_call" | custom-call | tf_op jit(solution)/shard_map/factor/pallas_call | solution.py:331
  22.9 2.0 %apply.1 = (bf16[1,8192,128]{2,1,0:T(8,128)(2,1)}, f32[1,8192]{1,0:T(1,128)}) custom-call(bf16[1,8192,128]{2,1,0:T(8,128)(2,1)S(1)} %get-tuple-element.6.anom_ref, bf16[2,128,128]{2,1,0:T(8,128)(2,1)S(1)} %get-tuple-element.8.total_ref, bf16[2,16,128]{2,1,0:T(8,128)(2,1)S(1)} %get-tuple-element.9.offset_ref), custom_call_target="tpu_custom_call" | custom-call | tf_op jit(solution)/shard_map/apply/pallas_call | solution.py:354

commit v2 on v1

--- a/solution.py
+++ b/solution.py
@@ -32,15 +32,15 @@
         lax.fori_loop(low, high, lambda k, c: (body(k), c)[1], 0)
 
 
-def fold(gram, two):
-    half = gram.shape[0] // 2
-    wide = gram.shape[1]
-    row = lax.broadcasted_iota(jnp.int32, (half, wide), 0)
-    lane = lax.broadcasted_iota(jnp.int32, (half, wide), 1)
-    low = gram[half:, :]
-    main = jnp.where((lane > row) & (lane < half), pltpu.roll(low, half, 1), gram[0:half, :])
-    diag = jnp.sum(jnp.where(lane == row + half, low, 0.0), axis=0, keepdims=True)
-    return main, jnp.where(lax.broadcasted_iota(jnp.int32, (PAD, wide), 0) == PAD - 1, diag, two)
+def fold(both, members):
+    row = lax.broadcasted_iota(jnp.int32, (members, members), 0)
+    col = lax.broadcasted_iota(jnp.int32, (members, members), 1)
+    one, two = both[0:members, 0:members], both[0:members, members:]
+    diag = jnp.sum(jnp.where(row == col, two, 0.0), axis=0, keepdims=True)
+    place = lax.broadcasted_iota(jnp.int32, (PAD, members), 0)
+    drives = both[members:members + PAD, :]
+    rest = jnp.where(place < 2, drives[:, 0:members], jnp.where(place < 4, pltpu.roll(drives[:, members:], 2, 0), diag))
+    return jnp.where(col > row, two, one), rest
 
 
 def gram_kernel(n, rows_hbm, weight_hbm, innov_hbm, block_hbm, anom_ref, out_ref, anom_out, anom_sem, rows_ref, weight_ref, innov_ref, block_ref, in_sem, scaled, drv, right, near, own, near_in, far_in, send_sem, recv_sem):
@@ -54,7 +54,6 @@
         load.start()
     me = lax.axis_index("space")
     members = rows_ref.shape[1]
-    half = members // 2
     chips = n // 2
     barrier = pltpu.get_barrier_semaphore()
 
@@ -89,11 +88,7 @@
         both = lax.dot_general(jnp.concatenate(lhs, axis=0), right[...], NT_DIMS, preferred_element_type=jnp.float32)
         for i in range(len(devs)):
             at = i * (members + 2 * PAD)
-            yield [
-                fold(both[at:at + members, members * h:members * (h + 1)],
-                     both[at + members:at + members + PAD, members * h:members * (h + 1)])
-                for h in range(BLK_DEV)
-            ]
+            yield fold(both[at:at + members + PAD, :], members)
 
     def near_copy(q):
         return pltpu.make_async_remote_copy(
@@ -109,9 +104,8 @@
 
     def work(q):
         for place, part in zip((near, own), parts((partner(me, 2 * q + 1, n), partner(me, 2 * q, n)))):
-            for h, (main, rest) in enumerate(part):
-                place[q, h, 0:half, :] = main
-                place[q, h, half:, :] = rest
+            place[q, 0:members, :] = part[0]
+            place[q, members:, :] = part[1]
 
     def relay(q):
         near_copy(q).wait()
@@ -126,9 +120,14 @@
         q = chips - 1 - turn
         work(q)
         near_copy(q).start()
-        relay(q + 1)
+        if chips > 16:
+            relay(q + 1)
+        elif turn > 1:
+            relay(q + 2)
 
     steps(1, chips, advance)
+    if 1 < chips <= 16:
+        relay(1)
     near_copy(0).wait()
     out_ref[...] = own[0] + near_in[0]
 
@@ -150,29 +149,34 @@
 
     steps(1, n, greet)
     members = tri.shape[1]
-    half = members // 2
     groups = members // 8
     lane = lax.broadcasted_iota(jnp.int32, (8, members), 1)
     sub_wide = lax.broadcasted_iota(jnp.int32, (8, members), 0)
     row = lax.broadcasted_iota(jnp.int32, (members, members), 0)
     col = lax.broadcasted_iota(jnp.int32, (members, members), 1)
+    main, rest = sums_ref[0:members, :], sums_ref[members:, :]
+    main_t = main.T
     work, drive = [], []
     for h in range(BLK_DEV):
-        main = sums_ref[h, 0:half, :]
-        rest = sums_ref[h, half:, :]
-        r0, c0 = row[0:half, :], col[0:half, :]
-        top = jnp.where((c0 < r0) | (c0 >= half), main, 0.0)
-        bottom = jnp.where(c0 > r0 + half, pltpu.roll(main, half, 1), 0.0)
-        part = jnp.concatenate([top, bottom], axis=0)
-        first = jnp.concatenate([main, jnp.broadcast_to(rest[PAD - 1:PAD, :], (half, members))], axis=0)
-        system = part + part.T + jnp.where(row == col, first + (members - 1.0), 0.0)
+        keep = col < row if h == 0 else col > row
+        line = main if h == 0 else jnp.broadcast_to(rest[2 * BLK_DEV:2 * BLK_DEV + 1, :], (members, members))
+        system = jnp.where(row == col, line + (members - 1.0), jnp.where(keep, main, main_t))
         work.append([system[8 * g:8 * g + 8, :] for g in range(groups)])
-        drive.append(rest[0:1, :] + rest[1:2, :])
-    inverse = [[], []]
+        drive.append(rest[2 * h:2 * h + 1, :] + rest[2 * h + 1:2 * h + 2, :])
+    inverse = [[] for _ in range(BLK_DEV)]
+    head = [None] * BLK_DEV
     for g0 in range(groups):
         base = 8 * g0
+        first = g0 % 2 == 0
         place = sub_wide + base
         panel = (lane >= base) & (lane < base + 8)
+
+        def drop(target, z):
+            terms = [target[:, base + q:base + q + 1] * z[q:q + 1, :] for q in range(8)]
+            while len(terms) > 1:
+                terms = [terms[i] + terms[i + 1] for i in range(0, len(terms), 2)]
+            return jnp.where(panel, 0.0, target) - terms[0]
+
         for h in range(BLK_DEV):
             w = work[h]
             z = jnp.where(panel, jnp.where(lane == place, 1.0, 0.0), w[g0])
@@ -182,26 +186,30 @@
                 here_row = sub_wide == q
                 kept = jnp.where(here_row, z, kept)
                 pivots = jnp.where(here_row, cols[q], pivots)
-                factor = jnp.where(here_row, 0.0, cols[q] * (1.0 / cols[q][q:q + 1, :]))
+                factor = jnp.where(here_row, 0.0, cols[q]) * (1.0 / cols[q][q:q + 1, :])
                 z = z - factor * z[q:q + 1, :]
                 for p in range(q + 1, 8):
                     cols[p] = cols[p] - factor * cols[p][q:q + 1, :]
             z = z * (1.0 / pivots)
             inverse[h].append(jnp.where(lane <= place, kept, 0.0) * lax.rsqrt(pivots))
-            if g0 + 1 == groups:
-                continue
-            fresh = jnp.where(panel, 0.0, w[g0 + 1])
-            for q in range(8):
-                fresh = fresh - w[g0 + 1][:, base + q:base + q + 1] * z[q:q + 1, :]
-            if g0 + 2 < groups:
-                rest = jnp.concatenate(w[g0 + 2:], axis=0)
-                wide = (col >= base)[0:members - base - 16, :] & (col < base + 8)[0:members - base - 16, :]
-                deep = jnp.concatenate([jnp.zeros((8, members), jnp.float32)] * g0 + [z] + [jnp.zeros((8, members), jnp.float32)] * (groups - g0 - 1), axis=0)
+            near = range(g0 + 1, min(groups, g0 + (4 if first else 3)))
+            old = w[g0 + 3:]
+            if first:
+                head[h] = z
+            elif old:
+                rest = jnp.concatenate(old, axis=0)
+                count = rest.shape[0]
+                wide = (col >= base - 8)[0:count, :] & (col < base + 8)[0:count, :]
+                above = [jnp.zeros((8, members), jnp.float32)] * (g0 - 1)
+                below = [jnp.zeros((8, members), jnp.float32)] * (groups - g0 - 1)
+                deep = jnp.concatenate(above + [drop(head[h], z), z] + below, axis=0)
                 moved = jnp.dot(jnp.where(wide, rest, 0.0), deep, precision=lax.Precision.HIGHEST, preferred_element_type=jnp.float32)
                 rest = jnp.where(wide, 0.0, rest) - moved
-                for g in range(g0 + 2, groups):
-                    w[g] = rest[8 * (g - g0 - 2):8 * (g - g0 - 1), :]
-            w[g0 + 1] = fresh
+            for g in near:
+                w[g] = drop(w[g], z)
+            if not first and old:
+                for g in range(g0 + 3, groups):
+                    w[g] = rest[8 * (g - g0 - 3):8 * (g - g0 - 2), :]
     scale = math.sqrt(members - 1.0)
     packed, lines = jnp.zeros((members, members), jnp.float32), []
     for h in range(BLK_DEV):
@@ -301,12 +309,12 @@
     count, members = obs_rows.shape[1:]
     n_space = lax.axis_size("space")
     n_time = lax.axis_size("tm")
-    wide = members // 2 + PAD
+    wide = members + PAD
     vmem = pl.BlockSpec(memory_space=pltpu.VMEM)
     sums, anom = pl.pallas_call(
         functools.partial(gram_kernel, n_space),
         out_shape=(
-            pltpu.VMEM((BLK_DEV, wide, members), jnp.float32),
+            pltpu.VMEM((wide, members), jnp.float32),
             pltpu.VMEM(state_anom.shape, state_anom.dtype),
         ),
         in_specs=[pl.BlockSpec(memory_space=pltpu.MemorySpace.HBM)] * 5,
@@ -321,7 +329,7 @@
             pltpu.VMEM((members, count), jnp.bfloat16),
             pltpu.VMEM((2 * PAD, count), jnp.bfloat16),
             pltpu.VMEM((BLK_DEV * members, count), jnp.bfloat16),
-            *[pltpu.VMEM((n_space // 2, BLK_DEV, wide, members), jnp.float32)] * 4,
+            *[pltpu.VMEM((n_space // 2, wide, members), jnp.float32)] * 4,
             pltpu.SemaphoreType.DMA((2, n_space // 2)),
             pltpu.SemaphoreType.DMA((2, n_space // 2)),
         ],

time: 25.1 us -> 24.4 us (0.972)
  Pallas kernels: 24.3 us -> 23.6 us
    pallas_call x1, Pallas kernels: 10.9 us -> 10.4 us  [body(): pl.pallas_call(functools.partial(factor_kernel, n_time), out_shape=(pltpu...]
where the time goes in v2:
time: 24.4 us; the launch traced here: 24.2 us
  Pallas kernels  23.6 us (97%)
  between operations  0.65 us (3%)
    pallas_call x1, Pallas kernels, body(): pl.pallas_call(functools.partial(gram_kernel, n_space), out_shape=(pltpu....  11.2 us
    pallas_call x1, Pallas kernels, body(): pl.pallas_call(functools.partial(factor_kernel, n_time), out_shape=(pltpu...  10.4 us
    pallas_call x1, Pallas kernels, body(): pl.pallas_call(apply_kernel, out_shape=(jax.ShapeDtypeStruct((1, rows_dev...  2.01 us

profile of v2, /device:TPU:0, one launch (start us, length us, event | category | flops | bytes accessed | tf_op | source)
XLA Modules:
  0.0 24.2 jit_solution(9161936200477572254)
XLA Ops:
  0.6 11.2 %gram.1 = (f32[136,128]{1,0:T(8,128)S(1)}, bf16[1,8192,128]{2,1,0:T(8,128)(2,1)S(1)}) custom-call(bf16[2048,128]{1,0:T(8,128)(2,1)} %bitcast.2, bf16[1,2048]{1,0:T(2,128)(2,1)} %weight_hbm.1, bf16[1,2048]{1,0:T(2,128)(2,1)} %innov_hbm.1, s32[1,2048]{1,0:T(1,128)} %bitcast.3, bf16[1,8192,128]{2,1,0:T(8,128)(2,1)} %anom_ref.1), custom_call_target="tpu_custom_call" | custom-call | tf_op jit(solution)/shard_map/gram/pallas_call | solution.py:314
  11.8 10.4 %factor.1 = (bf16[2,128,128]{2,1,0:T(8,128)(2,1)S(1)}, bf16[2,16,128]{2,1,0:T(8,128)(2,1)S(1)}) custom-call(f32[136,128]{1,0:T(8,128)S(1)} %get-tuple-element.7.sums_ref), custom_call_target="tpu_custom_call" | custom-call | tf_op jit(solution)/shard_map/factor/pallas_call | solution.py:339
  22.2 2.0 %apply.1 = (bf16[1,8192,128]{2,1,0:T(8,128)(2,1)}, f32[1,8192]{1,0:T(1,128)}) custom-call(bf16[1,8192,128]{2,1,0:T(8,128)(2,1)S(1)} %get-tuple-element.6.anom_ref, bf16[2,128,128]{2,1,0:T(8,128)(2,1)S(1)} %get-tuple-element.8.total_ref, bf16[2,16,128]{2,1,0:T(8,128)(2,1)S(1)} %get-tuple-element.9.offset_ref), custom_call_target="tpu_custom_call" | custom-call | tf_op jit(solution)/shard_map/apply/pallas_call | solution.py:362

commit v3 on v2

--- a/solution.py
+++ b/solution.py
@@ -67,9 +67,8 @@
     for load in loads:
         load.wait()
     weight = weight_ref[...].astype(jnp.float32)
-    rows_t = rows_ref[...].astype(jnp.float32).T
-    scaled[...] = (weight * rows_t).astype(jnp.bfloat16)
-    rows_t = rows_t.astype(jnp.bfloat16)
+    rows_t = rows_ref[...].T
+    scaled[...] = (weight * rows_t.astype(jnp.float32)).astype(jnp.bfloat16)
     for h in range(BLK_DEV):
         pick = jnp.where(block_ref[...] % BLK_DEV == h, 1.0, 0.0).astype(jnp.bfloat16)
         right[members * h:members * (h + 1), :] = rows_t * pick

time: 24.4 us -> 24.4 us (level)
  no operation moved by 1% of the time
where the time goes in v3:
time: 24.4 us; the launch traced here: 24.2 us
  Pallas kernels  23.6 us (97%)
  between operations  0.65 us (3%)
    pallas_call x1, Pallas kernels, body(): pl.pallas_call(functools.partial(gram_kernel, n_space), out_shape=(pltpu....  11.1 us
    pallas_call x1, Pallas kernels, body(): pl.pallas_call(functools.partial(factor_kernel, n_time), out_shape=(pltpu...  10.4 us
    pallas_call x1, Pallas kernels, body(): pl.pallas_call(apply_kernel, out_shape=(jax.ShapeDtypeStruct((1, rows_dev...  2.01 us

profile of v3, /device:TPU:0, one launch (start us, length us, event | category | flops | bytes accessed | tf_op | source)
XLA Modules:
  0.0 24.2 jit_solution(1144333088859838501)
XLA Ops:
  0.6 11.1 %gram.1 = (f32[136,128]{1,0:T(8,128)S(1)}, bf16[1,8192,128]{2,1,0:T(8,128)(2,1)S(1)}) custom-call(bf16[2048,128]{1,0:T(8,128)(2,1)} %bitcast.2, bf16[1,2048]{1,0:T(2,128)(2,1)} %weight_hbm.1, bf16[1,2048]{1,0:T(2,128)(2,1)} %innov_hbm.1, s32[1,2048]{1,0:T(1,128)} %bitcast.3, bf16[1,8192,128]{2,1,0:T(8,128)(2,1)} %anom_ref.1), custom_call_target="tpu_custom_call" | custom-call | tf_op jit(solution)/shard_map/gram/pallas_call | solution.py:313
  11.8 10.4 %factor.1 = (bf16[2,128,128]{2,1,0:T(8,128)(2,1)S(1)}, bf16[2,16,128]{2,1,0:T(8,128)(2,1)S(1)}) custom-call(f32[136,128]{1,0:T(8,128)S(1)} %get-tuple-element.7.sums_ref), custom_call_target="tpu_custom_call" | custom-call | tf_op jit(solution)/shard_map/factor/pallas_call | solution.py:338
  22.2 2.0 %apply.1 = (bf16[1,8192,128]{2,1,0:T(8,128)(2,1)}, f32[1,8192]{1,0:T(1,128)}) custom-call(bf16[1,8192,128]{2,1,0:T(8,128)(2,1)S(1)} %get-tuple-element.6.anom_ref, bf16[2,128,128]{2,1,0:T(8,128)(2,1)S(1)} %get-tuple-element.8.total_ref, bf16[2,16,128]{2,1,0:T(8,128)(2,1)S(1)} %get-tuple-element.9.offset_ref), custom_call_target="tpu_custom_call" | custom-call | tf_op jit(solution)/shard_map/apply/pallas_call | solution.py:361
